TPU v7x, 256 devices: a whole 4x4x8 slice. The times are simulated.
256 devices in a mesh: rows: 32 (over z, x), cols: 8 (over y, core).
Axes of the slice: x: 4, y: 4, z: 8, core: 2. Of those that a mesh axis runs over, the one named last changes fastest.
Arguments:
- block_values: bfloat16 [256, 256, 128, 128], P('rows', 'cols')
- block_columns: int32 [256, 256], P('rows', 'cols'), may hold values from 0 to 1023, as said below
- row_counts: int32 [256, 8], P('rows', 'cols'), may hold values from 1 to 32, as said below
- sketch: bfloat16 [1048576, 256], P(('rows', 'cols')), may hold values from -6 to 6
Outputs:
- basis: float32 [32768, 256], P(('rows', 'cols'))
- triangle: float32 [256, 256], replicated
Inputs may be any that keep to these rules, and one draw needn't show every extreme that they name: row_counts[b, c] counts the live slots among slots c * 32 to c * 32 + 31 of block-row b; some entry equals 32. `block_columns`: take the 8 x 32 slots of one index of rows and one column group c; among them at most 12 name block-columns j with the same j // 32, and in every such set some j // 32 is named by exactly 12 slots.
All inputs are finite; a program needn't handle non-finite values.
Results may differ from a plain program's by a relative error of at most 0.0003.
Values may be sent and summed in bfloat16 or wider, within the bound.
No kernel may reach another device: no remote copies, remote signals or barrier semaphores. Data moves between devices by JAX's collectives and lax.ppermute only.
A program may use at most 128 MiB of HBM per device.

v0:
```python
import jax
import jax.numpy as jnp
from jax import lax
from jax.sharding import PartitionSpec as P


def request_table(columns_flat, per_owner, axis_rows, capacity):
    owners = columns_flat // per_owner
    onehot = (owners[:, None] == jnp.arange(axis_rows, dtype=jnp.int32)[None, :]).astype(jnp.int32)
    before = jnp.cumsum(onehot, axis=0) - onehot
    ranking = jnp.sum(before * onehot, axis=1)
    position = owners * capacity + ranking
    wanted = (
        jnp.zeros((axis_rows * capacity,), jnp.int32).at[position].set(columns_flat % per_owner)
    )
    return (position, wanted.reshape(axis_rows, capacity))


def send_back(wanted, local_blocks):
    blocks = local_blocks[wanted]
    return lax.all_to_all(blocks, "rows", split_axis=0, concat_axis=0, tiled=True)


def row_products(values_rows, positions_rows, counts_rows, table):
    slot_count = values_rows.shape[1]
    slot_ids = jnp.arange(slot_count, dtype=jnp.int32)

    def one_row(entries):
        values_row, positions_row, counts_row = entries
        picked = table[positions_row]
        live_mask = (slot_ids < counts_row[0]).astype(jnp.bfloat16)
        picked = picked * live_mask[:, None, None]
        return jnp.einsum("sab,sbk->ak", values_row, picked, preferred_element_type=jnp.float32)

    result = lax.map(one_row, (values_rows, positions_rows, counts_rows))
    return result.reshape(-1, table.shape[2])


def per_device(block_values, block_columns, row_counts, sketch):
    block_order = block_values.shape[2]
    sketch_width = sketch.shape[1]
    axis_rows = lax.axis_size("rows")
    slot_total = block_columns.shape[0] * block_columns.shape[1]
    capacity = 3 * slot_total // (2 * axis_rows)
    local_blocks = sketch.reshape(-1, block_order, sketch_width)
    per_owner = local_blocks.shape[0]
    position, wanted_here = request_table(block_columns.reshape(-1), per_owner, axis_rows, capacity)
    table = send_back(
        lax.all_to_all(wanted_here, "rows", split_axis=0, concat_axis=0, tiled=True), local_blocks
    )
    table = table.reshape(-1, block_order, sketch_width)
    positions = position.reshape(block_columns.shape[0], block_columns.shape[1])
    partial_image = row_products(block_values, positions, row_counts, table)
    image_here = lax.psum_scatter(partial_image, "cols", scatter_dimension=0, tiled=True)
    total_rows = image_here.shape[0] * lax.axis_size("rows") * lax.axis_size("cols")
    gram_local = jnp.dot(
        image_here.T,
        image_here,
        precision=lax.Precision.HIGHEST,
        preferred_element_type=jnp.float32,
    )
    gram_matrix = lax.psum(gram_local, ("rows", "cols")) / total_rows
    lower_factor = jnp.linalg.cholesky(gram_matrix)
    basis_rows = jax.scipy.linalg.solve_triangular(lower_factor, image_here.T, lower=True).T
    return (basis_rows, lower_factor.T)


def solution(mesh):
    return jax.shard_map(
        per_device,
        mesh=mesh,
        in_specs=(
            P("rows", "cols", None, None),
            P("rows", "cols"),
            P("rows", "cols"),
            P(("rows", "cols"), None),
        ),
        out_specs=(P(("rows", "cols"), None), P()),
        check_vma=False,
    )
```

profile of v0, /device:TPU:2, one launch (start us, length us, event | category | flops | bytes accessed | tf_op | source)
XLA Modules:
  0.0 1127.3 jit_solution(16945406172135663035)
XLA Ops:
  7.2 0.9 reshape.225
  8.1 0.8 reshape.224
  8.9 0.8 reshape.228
  9.6 0.6 reduce-window.6
  10.6 1.4 scatter_custom_fusion
  12.1 20.0 %all_to_all.17 = s32[32,1,12]{2,1,0:T(1,128)S(1)} all-to-all(s32[32,1,12]{2,1,0:T(1,128)S(1)} %bitcast.99), channel_id=1, replica_groups=mesh['rows'=32,'cols'=8] {'rows'}, dimensions={0} | all-to-all | bytes 3072 | tf_op jit(solution)/shard_map/all_to_all | solution.py:49
  32.2 12.9 %gather_fusion.1 = bf16[384,128,256]{2,1,0:T(8,128)(2,1)} fusion(bf16[32,128,256]{2,1,0:T(8,128)(2,1)S(1)} %bitcast.94, s32[1024]{0:T(1024)S(1)} %pad_clamp_fusion.1), kind=kCustom, calls=%fused_computation.1 | custom fusion | bytes 50333184 | tf_op jit(solution)/shard_map/gather | solution.py:20
  45.1 6.5 all-to-all-start.1
  51.7 577.4 %all-to-all-done.1 = bf16[32,12,128,256]{3,2,1,0:T(8,128)(2,1)} async-done(((bf16[32,12,128,256]{3,2,1,0:T(8,128)(2,1)}), bf16[32,12,128,256]{3,2,1,0:T(8,128)(2,1)}, u32[]{:S(2)}, u32[]{:S(2)}) %all-to-all-start.1) | async-done | bytes 25165856 | tf_op jit(solution)/shard_map/all_to_all | solution.py:21
  629.1 95.0 %while.13 = (s32[]{:T(128)}, f32[8,128,256]{2,1,0:T(8,128)S(1)}, bf16[8,32,128,128]{3,2,1,0:T(8,128)(2,1)}, s32[8,32]{1,0:T(8,128)S(1)}, bf16[384,128,256]{2,1,0:T(8,128)(2,1)}, /*index=5*/s32[8,1]{0,1:T(1,128)S(1)}, s32[]{:T(128)}) while((s32[]{:T(128)}, f32[8,128,256]{2,1,0:T(8,128)S(1)}, bf16[8,32,128,128]{3,2,1,0:T(8,128)(2,1)}, ...), condition=%wide.region_5.6_spmd.clone, body=%wide.region_4.5_spmd.clone.sunk | while | flops 269485216 | bytes 7477409 | solution.py:35
  629.1 8.8 gather_fusion
  638.0 0.6 constant_dynamic-slice_fusion.6
  638.6 0.6 compare_convert_fusion.2
  639.2 1.8 fusion.53
  641.0 8.8 gather_fusion
  649.8 0.6 constant_dynamic-slice_fusion.6
  650.4 0.6 compare_convert_fusion.2
  651.1 1.8 fusion.53
  652.9 8.8 gather_fusion
  661.7 0.6 constant_dynamic-slice_fusion.6
  662.3 0.6 compare_convert_fusion.2
  663.0 1.8 fusion.53
  664.8 8.8 gather_fusion
  673.6 0.6 constant_dynamic-slice_fusion.6
  674.2 0.6 compare_convert_fusion.2
  674.8 1.8 fusion.53
  676.6 8.8 gather_fusion
  685.5 0.6 constant_dynamic-slice_fusion.6
  686.1 0.6 compare_convert_fusion.2
  686.7 1.8 fusion.53
  688.5 8.8 gather_fusion
  697.4 0.6 constant_dynamic-slice_fusion.6
  698.0 0.6 compare_convert_fusion.2
  698.6 1.8 fusion.53
  700.4 8.8 gather_fusion
  709.3 0.6 constant_dynamic-slice_fusion.6
  709.9 0.6 compare_convert_fusion.2
  710.5 1.8 fusion.53
  712.3 8.8 gather_fusion
  721.1 0.6 constant_dynamic-slice_fusion.6
  721.7 0.6 compare_convert_fusion.2
  722.4 1.8 fusion.53
  724.1 1.3 copy.23
  725.5 0.2 all-reduce.3.cloned.1.call-start
  725.7 70.9 %reduce-scatter.2.cloned.1.call-done = f32[128,256]{0,1:T(8,128)} async-done(((f32[1024,256]{0,1:T(8,128)}), f32[128,256]{0,1:T(8,128)}) %reduce-scatter.2.cloned.1.call-update) | async-done | bytes 131088 | tf_op jit(solution)/shard_map/reduce_scatter | solution.py:54
  796.6 2.1 fusion.37
  798.7 257.2 %all-reduce.3.cloned.1.call-done = f32[256,256]{0,1:T(8,128)} async-done(((f32[256,256]{0,1:T(8,128)}), f32[256,256]{0,1:T(8,128)}) %all-reduce.3.cloned.1.call-update) | async-done | bytes 262160 | tf_op jit(solution)/shard_map/psum | solution.py:62
  1055.9 1.0 broadcast_multiply_fusion
  1057.0 1.0 fusion.16
  1058.0 11.7 %cholesky.50 = f32[128,128]{1,0:T(8,128)S(1)} custom-call(f32[128,128]{1,0:T(8,128)S(1)} %cholesky.118), custom_call_target="Cholesky" | custom-call | tf_op jit(solution)/shard_map/jit(cholesky)/cholesky | solution.py:63
  1069.8 9.8 custom-call.15
  1079.8 0.3 convolution_subtract_fusion.1
  1080.1 11.7 %cholesky.105 = f32[128,128]{1,0:T(8,128)S(1)} custom-call(f32[128,128]{1,0:T(8,128)S(1)} %convolution_subtract_fusion.1), custom_call_target="Cholesky" | custom-call | tf_op jit(solution)/shard_map/jit(cholesky)/cholesky | solution.py:63
  1091.9 0.7 compare_reduce_fusion
  1094.0 4.3 while.12
  1094.2 0.6 fusion.49
  1094.8 1.4 bitcast_dynamic-update-slice_fusion.2
  1096.3 0.6 fusion.49
  1096.9 1.4 bitcast_dynamic-update-slice_fusion.2
  1098.3 19.7 %custom-call.16 = f32[2,128,128]{1,2,0:T(8,128)S(1)} custom-call(f32[2,128,128]{2,1,0:T(8,128)S(1)} %get-tuple-element.47), custom_call_target="InvertDiagBlocksLowerTriangular" | custom-call | tf_op jit(solution)/shard_map/jit(_solve_triangular)/triangular_solve | solution.py:64
  1118.0 0.3 fusion.21
  1118.5 0.3 fusion.20
  1118.8 0.8 copy.20
  1119.6 0.8 copy.21
  (58 shorter events, 1.7 us)
Async XLA Ops:
  7.2 25.0 %copy-start = (bf16[4096,256]{1,0:T(8,128)(2,1)S(1)}, bf16[4096,256]{1,0:T(8,128)(2,1)}, u32[]{:S(2)}) copy-start(bf16[4096,256]{1,0:T(8,128)(2,1)} %param.9) | copy-start | bytes 6291460
  45.1 6.6 copy-start.3
  45.1 584.0 %copy-start.4 = (s32[8,1]{0,1:T(1,128)S(1)}, s32[8,1]{0,1:T(1,128)}, u32[]{:S(2)}) copy-start(s32[8,1]{0,1:T(1,128)} %param.8) | copy-start | bytes 100
  45.1 584.0 %all-to-all-start.1 = ((bf16[32,12,128,256]{3,2,1,0:T(8,128)(2,1)}), bf16[32,12,128,256]{3,2,1,0:T(8,128)(2,1)}, u32[]{:S(2)}, u32[]{:S(2)}) async-start(bf16[32,12,128,256]{3,2,1,0:T(8,128)(2,1)} %bitcast.95), calls=%async_computation.1 | async-start | bytes 50331648 | tf_op jit(solution)/shard_map/all_to_all | solution.py:21
  51.6 745.0 %reduce-scatter.2.cloned.1.call-start = ((), (), s32[]{:S(2)}) async-start(), calls=%async_computation.3 | async-start | bytes 1179648 | tf_op jit(solution)/shard_map/reduce_scatter | solution.py:54
  725.5 330.4 %all-reduce.3.cloned.1.call-start = ((), (), s32[]{:S(2)}) async-start(), calls=%async_computation.4 | async-start | bytes 524288 | tf_op jit(solution)/shard_map/psum | solution.py:62
  1056.9 61.1 %copy-start.2 = (f32[128,256]{0,1:T(8,128)S(1)}, f32[128,256]{0,1:T(8,128)}, u32[]{:S(2)}) copy-start(f32[128,256]{0,1:T(8,128)} %reduce-scatter.2.cloned.1.call-done) | copy-start | bytes 393220
  1069.8 50.6 %copy-start.1 = (bf16[4096,256]{1,0:T(8,128)(2,1)S(1)}, bf16[4096,256]{1,0:T(8,128)(2,1)}, u32[]{:S(2)}) copy-start(bf16[4096,256]{1,0:T(8,128)(2,1)} %param.9) | copy-start | bytes 6291460
Sparse Core Ops, SparseCore 0:
  725.6 70.9 reduce-scatter.1
  802.6 253.2 all-reduce.2
where the time goes:
time: 1130 us
  waiting for transfers between devices  905 us (80%)
  local copies, waits for them, and re-layouts  99.9 us (9%)
  other arithmetic  61.6 us (5%)
  blocking collectives  20 us (2%)
  matrix products  17.3 us (2%)
  between operations  15.6 us (1%)
    all_to_all x1, waiting for transfers between devices, send_back(): lax.all_to_all(blocks, 'rows', split_axis=0, concat_axis=0, tiled=True)  577 us
    psum x1, waiting for transfers between devices, per_device(): gram_matrix = lax.psum(gram_local, ('rows', 'cols')) / total_rows  257 us
    reduce_scatter x1, waiting for transfers between devices, per_device(): lax.psum_scatter(partial_image, 'cols', scatter_dimension=0, tiled=True)  70.9 us
    gather x8, local copies, waits for them, and re-layouts, one_row(): picked = table[positions_row]  70.7 us
    another operation x6, other arithmetic, per_device(): lower_factor = jnp.linalg.cholesky(gram_matrix)  34 us
  transfers between devices with their start and end apart: 3, of which 3 were waited for; matrix products, arithmetic and copies ran while one was open for 0% of the time, Pallas kernels for 0%

commit v1 on v0

--- a/solution.py
+++ b/solution.py
@@ -59,7 +59,7 @@
         precision=lax.Precision.HIGHEST,
         preferred_element_type=jnp.float32,
     )
-    gram_matrix = lax.psum(gram_local, ("rows", "cols")) / total_rows
+    gram_matrix = lax.psum(lax.psum(gram_local, "cols"), "rows") / total_rows
     lower_factor = jnp.linalg.cholesky(gram_matrix)
     basis_rows = jax.scipy.linalg.solve_triangular(lower_factor, image_here.T, lower=True).T
     return (basis_rows, lower_factor.T)

time: 1130 us -> 1080 us (0.956)
  waiting for transfers between devices: 905 us -> 860 us
    psum x1 -> x2, waiting for transfers between devices: 257 us -> 212 us  [per_device(): gram_matrix = lax.psum(lax.psum(gram_local, 'cols'), 'rows') / total_rows]
  transfers between devices with their start and end apart: 3 -> 4, of which waited for: 3 -> 4; matrix products, arithmetic and copies ran while one was open for 0% -> 0% of each run, Pallas kernels for 0% -> 0%
where the time goes in v1:
time: 1080 us
  waiting for transfers between devices  860 us (80%)
  local copies, waits for them, and re-layouts  99.9 us (9%)
  other arithmetic  61.6 us (6%)
  blocking collectives  20 us (2%)
  matrix products  17.3 us (2%)
  between operations  15.3 us (1%)
    all_to_all x1, waiting for transfers between devices, send_back(): lax.all_to_all(blocks, 'rows', split_axis=0, concat_axis=0, tiled=True)  577 us
    psum x2, waiting for transfers between devices, per_device(): gram_matrix = lax.psum(lax.psum(gram_local, 'cols'), 'rows') / total_rows  212 us
    reduce_scatter x1, waiting for transfers between devices, per_device(): lax.psum_scatter(partial_image, 'cols', scatter_dimension=0, tiled=True)  71.1 us
    gather x8, local copies, waits for them, and re-layouts, one_row(): picked = table[positions_row]  70.7 us
    another operation x6, other arithmetic, per_device(): lower_factor = jnp.linalg.cholesky(gram_matrix)  34 us
  transfers between devices with their start and end apart: 4, of which 4 were waited for; matrix products, arithmetic and copies ran while one was open for 0% of the time, Pallas kernels for 0%

profile of v1, /device:TPU:2, one launch (start us, length us, event | category | flops | bytes accessed | tf_op | source)
XLA Modules:
  0.0 1081.9 jit_solution(9314899777730781380)
XLA Ops:
  7.2 0.9 reshape.225
  8.1 0.8 reshape.224
  8.9 0.8 reshape.228
  9.6 0.6 reduce-window.6
  10.6 1.4 scatter_custom_fusion
  12.1 20.0 %all_to_all.17 = s32[32,1,12]{2,1,0:T(1,128)S(1)} all-to-all(s32[32,1,12]{2,1,0:T(1,128)S(1)} %bitcast.99), channel_id=1, replica_groups=mesh['rows'=32,'cols'=8] {'rows'}, dimensions={0} | all-to-all | bytes 3072 | tf_op jit(solution)/shard_map/all_to_all | solution.py:49
  32.2 12.9 %gather_fusion.1 = bf16[384,128,256]{2,1,0:T(8,128)(2,1)} fusion(bf16[32,128,256]{2,1,0:T(8,128)(2,1)S(1)} %bitcast.94, s32[1024]{0:T(1024)S(1)} %pad_clamp_fusion.1), kind=kCustom, calls=%fused_computation.1 | custom fusion | bytes 50333184 | tf_op jit(solution)/shard_map/gather | solution.py:20
  45.1 6.5 all-to-all-start.1
  51.7 577.4 %all-to-all-done.1 = bf16[32,12,128,256]{3,2,1,0:T(8,128)(2,1)} async-done(((bf16[32,12,128,256]{3,2,1,0:T(8,128)(2,1)}), bf16[32,12,128,256]{3,2,1,0:T(8,128)(2,1)}, u32[]{:S(2)}, u32[]{:S(2)}) %all-to-all-start.1) | async-done | bytes 25165856 | tf_op jit(solution)/shard_map/all_to_all | solution.py:21
  629.1 95.0 %while.13 = (s32[]{:T(128)}, f32[8,128,256]{2,1,0:T(8,128)S(1)}, bf16[8,32,128,128]{3,2,1,0:T(8,128)(2,1)}, s32[8,32]{1,0:T(8,128)S(1)}, bf16[384,128,256]{2,1,0:T(8,128)(2,1)}, /*index=5*/s32[8,1]{0,1:T(1,128)S(1)}, s32[]{:T(128)}) while((s32[]{:T(128)}, f32[8,128,256]{2,1,0:T(8,128)S(1)}, bf16[8,32,128,128]{3,2,1,0:T(8,128)(2,1)}, ...), condition=%wide.region_5.6_spmd.clone, body=%wide.region_4.5_spmd.clone.sunk | while | flops 269485216 | bytes 7477409 | solution.py:35
  629.1 8.8 gather_fusion
  638.0 0.6 constant_dynamic-slice_fusion.6
  638.6 0.6 compare_convert_fusion.2
  639.2 1.8 fusion.53
  641.0 8.8 gather_fusion
  649.8 0.6 constant_dynamic-slice_fusion.6
  650.4 0.6 compare_convert_fusion.2
  651.1 1.8 fusion.53
  652.9 8.8 gather_fusion
  661.7 0.6 constant_dynamic-slice_fusion.6
  662.3 0.6 compare_convert_fusion.2
  663.0 1.8 fusion.53
  664.8 8.8 gather_fusion
  673.6 0.6 constant_dynamic-slice_fusion.6
  674.2 0.6 compare_convert_fusion.2
  674.8 1.8 fusion.53
  676.6 8.8 gather_fusion
  685.5 0.6 constant_dynamic-slice_fusion.6
  686.1 0.6 compare_convert_fusion.2
  686.7 1.8 fusion.53
  688.5 8.8 gather_fusion
  697.4 0.6 constant_dynamic-slice_fusion.6
  698.0 0.6 compare_convert_fusion.2
  698.6 1.8 fusion.53
  700.4 8.8 gather_fusion
  709.3 0.6 constant_dynamic-slice_fusion.6
  709.9 0.6 compare_convert_fusion.2
  710.5 1.8 fusion.53
  712.3 8.8 gather_fusion
  721.1 0.6 constant_dynamic-slice_fusion.6
  721.7 0.6 compare_convert_fusion.2
  722.4 1.8 fusion.53
  724.1 1.3 copy.23
  725.5 71.1 %reduce-scatter.2.cloned.1.call-done = f32[128,256]{0,1:T(8,128)} async-done(((f32[1024,256]{0,1:T(8,128)}), f32[128,256]{0,1:T(8,128)}) %reduce-scatter.2.cloned.1.call-update) | async-done | bytes 131088 | tf_op jit(solution)/shard_map/reduce_scatter | solution.py:54
  796.6 2.1 fusion.37
  798.9 65.0 %all-reduce.4.cloned.1.call-done = f32[256,256]{0,1:T(8,128)} async-done(((f32[256,256]{0,1:T(8,128)}), f32[256,256]{0,1:T(8,128)}) %all-reduce.4.cloned.1.call-update) | async-done | bytes 262160 | tf_op jit(solution)/shard_map/psum | solution.py:62
  863.9 146.9 %all-reduce.6.cloned.1.call-done = f32[256,256]{0,1:T(8,128)} async-done(((f32[256,256]{0,1:T(8,128)}), f32[256,256]{0,1:T(8,128)}) %all-reduce.6.cloned.1.call-update) | async-done | bytes 262160 | tf_op jit(solution)/shard_map/psum | solution.py:62
  1010.8 1.0 broadcast_multiply_fusion
  1012.0 1.0 fusion.16
  1013.0 11.7 %cholesky.50 = f32[128,128]{1,0:T(8,128)S(1)} custom-call(f32[128,128]{1,0:T(8,128)S(1)} %cholesky.118), custom_call_target="Cholesky" | custom-call | tf_op jit(solution)/shard_map/jit(cholesky)/cholesky | solution.py:63
  1024.7 9.8 custom-call.15
  1034.8 0.3 convolution_subtract_fusion.1
  1035.0 11.7 %cholesky.105 = f32[128,128]{1,0:T(8,128)S(1)} custom-call(f32[128,128]{1,0:T(8,128)S(1)} %convolution_subtract_fusion.1), custom_call_target="Cholesky" | custom-call | tf_op jit(solution)/shard_map/jit(cholesky)/cholesky | solution.py:63
  1046.8 0.7 compare_reduce_fusion
  1049.0 4.3 while.12
  1049.2 0.6 fusion.49
  1049.8 1.4 bitcast_dynamic-update-slice_fusion.2
  1051.2 0.6 fusion.49
  1051.8 1.4 bitcast_dynamic-update-slice_fusion.2
  1053.3 19.7 %custom-call.16 = f32[2,128,128]{1,2,0:T(8,128)S(1)} custom-call(f32[2,128,128]{2,1,0:T(8,128)S(1)} %get-tuple-element.47), custom_call_target="InvertDiagBlocksLowerTriangular" | custom-call | tf_op jit(solution)/shard_map/jit(_solve_triangular)/triangular_solve | solution.py:64
  1072.9 0.3 fusion.21
  1073.5 0.3 fusion.20
  1073.8 0.8 copy.20
  1074.5 0.8 copy.21
  (61 shorter events, 1.9 us)
Async XLA Ops:
  7.2 25.0 %copy-start = (bf16[4096,256]{1,0:T(8,128)(2,1)S(1)}, bf16[4096,256]{1,0:T(8,128)(2,1)}, u32[]{:S(2)}) copy-start(bf16[4096,256]{1,0:T(8,128)(2,1)} %param.9) | copy-start | bytes 6291460
  45.1 6.6 copy-start.3
  45.1 584.0 %copy-start.4 = (s32[8,1]{0,1:T(1,128)S(1)}, s32[8,1]{0,1:T(1,128)}, u32[]{:S(2)}) copy-start(s32[8,1]{0,1:T(1,128)} %param.8) | copy-start | bytes 100
  45.1 584.0 %all-to-all-start.1 = ((bf16[32,12,128,256]{3,2,1,0:T(8,128)(2,1)}), bf16[32,12,128,256]{3,2,1,0:T(8,128)(2,1)}, u32[]{:S(2)}, u32[]{:S(2)}) async-start(bf16[32,12,128,256]{3,2,1,0:T(8,128)(2,1)} %bitcast.95), calls=%async_computation.1 | async-start | bytes 50331648 | tf_op jit(solution)/shard_map/all_to_all | solution.py:21
  51.6 745.0 %reduce-scatter.2.cloned.1.call-start = ((), (), s32[]{:S(2)}) async-start(), calls=%async_computation.3 | async-start | bytes 1179648 | tf_op jit(solution)/shard_map/reduce_scatter | solution.py:54
  725.5 138.4 %all-reduce.4.cloned.1.call-start = ((), (), s32[]{:S(2)}) async-start(), calls=%async_computation.4 | async-start | bytes 524288 | tf_op jit(solution)/shard_map/psum | solution.py:62
  798.7 212.2 %all-reduce.6.cloned.1.call-start = ((), (), s32[]{:S(2)}) async-start(), calls=%async_computation.5 | async-start | bytes 524288 | tf_op jit(solution)/shard_map/psum | solution.py:62
  1011.8 61.1 %copy-start.2 = (f32[128,256]{0,1:T(8,128)S(1)}, f32[128,256]{0,1:T(8,128)}, u32[]{:S(2)}) copy-start(f32[128,256]{0,1:T(8,128)} %reduce-scatter.2.cloned.1.call-done) | copy-start | bytes 393220
  1024.7 50.6 %copy-start.1 = (bf16[4096,256]{1,0:T(8,128)(2,1)S(1)}, bf16[4096,256]{1,0:T(8,128)(2,1)}, u32[]{:S(2)}) copy-start(bf16[4096,256]{1,0:T(8,128)(2,1)} %param.9) | copy-start | bytes 6291460
Sparse Core Ops, SparseCore 0:
  725.6 70.9 reduce-scatter.1
  799.5 64.3 all-reduce.3
  867.3 143.4 all-reduce.5
